TPU v7x, 256 devices: a whole 4x4x8 slice. The times are simulated.
256 devices in a mesh: row: 16 (over y, z_hi), col: 16 (over x, z_lo, core).
Axes of the slice: x: 4, y: 4, z: 8 (z_hi: 4, z_lo: 2; z = z_hi * 2 + z_lo), core: 2. Of those that a mesh axis runs over, the one named last changes fastest.
Arguments:
- fit_tiles: bfloat16 [32, 96, 128, 128], P('row', 'col'), may hold values from -6 to 6
- aux_list: int32 [32, 96], P('row', 'col'), may hold values from 0 to 11, as said below
- aux_count: int32 [32, 16], P('row', 'col'), may hold values from 1 to 6, as said below
- metric: bfloat16 [192, 128, 128], P('col', 'row'), may hold values from -0.5 to 0.5
Outputs:
- exchange: float32 [4096, 4096], P('col', 'row')
Inputs may be any that keep to these rules, and one draw needn't show every extreme that they name: `aux_list`: within one atom block and one col shard, the first 6 slots name distinct auxiliary blocks. `aux_count`: counts follow a density per atom block; the largest is reached in every draw.
All inputs are finite; a program needn't handle non-finite values.
Results may differ from a plain program's by a relative error of at most 0.0015.
Values may be sent and summed in bfloat16 or wider, within the bound.
No kernel may reach another device: no remote copies, remote signals or barrier semaphores. Data moves between devices by JAX's collectives and lax.ppermute only.
A program may use at most 64 MiB of HBM per device.

v0:
```python
import jax
import jax.numpy as jnp
from jax import lax
from jax.sharding import PartitionSpec as P

AUXB = 128
QS = 6


def expand(fitted, marked, local_aux):
    onehot = (marked[:, :, None] == jnp.arange(local_aux, dtype=jnp.int32)[None, None, :]).astype(
        jnp.bfloat16
    )
    dense = jnp.einsum("asq,asmn->amqn", onehot, fitted, preferred_element_type=jnp.float32).astype(
        jnp.bfloat16
    )
    return dense.reshape(fitted.shape[0] * fitted.shape[2], local_aux * fitted.shape[3])


def local(fit_tiles, aux_list, aux_count, metric):
    slots = fit_tiles.shape[1]
    local_aux = metric.shape[0]
    full_metric = lax.all_gather(metric, "row", axis=1, tiled=True)
    alive = jnp.arange(slots, dtype=jnp.int32)[None, :] < aux_count
    marked = jnp.where(alive, aux_list, local_aux)
    picked = full_metric[aux_list]
    fitted = jnp.einsum(
        "asmk,askn->asmn", fit_tiles, picked, preferred_element_type=jnp.float32
    ).astype(jnp.bfloat16)
    dense = expand(fitted, marked, local_aux)
    factor = 1.0 / (QS * lax.axis_size("col") * AUXB) ** 0.5
    gathered = lax.all_gather(dense, "row", axis=0, tiled=True)
    summed = lax.psum_scatter(
        jnp.dot(gathered, dense.T, preferred_element_type=jnp.float32),
        "col",
        scatter_dimension=0,
        tiled=True,
    )
    return summed * factor


def solution(mesh):
    placed = (P("row", "col", None, None), P("row", "col"), P("row", "col"), P("col", "row", None))
    return jax.shard_map(
        local, mesh=mesh, in_specs=placed, out_specs=P("col", "row"), check_vma=False
    )
```

profile of v0, /device:TPU:8, one launch (start us, length us, event | category | flops | bytes accessed | tf_op | source)
XLA Modules:
  0.0 312.3 jit_solution(8098111673905659290)
XLA Ops:
  6.5 0.0 copy-start
  6.5 0.0 all-gather.2.cloned.1.call-start
  6.5 0.8 compare_select_fusion.1
  7.3 0.1 reshape.7
  7.4 44.8 %all_gather.6 = bf16[12,128,128]{2,1,0:T(8,128)(2,1)S(1)} all-gather(bf16[12,8,128]{2,1,0:T(8,128)(2,1)} %param.7), channel_id=1, replica_groups=mesh['row'=16,'col'=16] {'row'}, dimensions={1}, use_global_device_ids=true | all-gather | bytes 417792 | tf_op jit(solution)/shard_map/all_gather | solution.py:23
  52.2 0.6 gather_fusion
  52.8 0.0 copy-done
  52.8 0.4 fusion.5
  53.3 0.3 copy.6
  53.6 0.6 convolution_convert_fusion
  54.1 0.2 copy.11
  54.3 1.2 copy.8
  55.6 0.0 all-gather.2.cloned.1.call-update
  55.6 0.0 reduce-scatter.2.cloned.1.call-start
  55.6 149.9 %all-gather.2.cloned.1.call-done = bf16[4096,1536]{0,1:T(8,128)(2,1)} async-done(((bf16[256,1536]{0,1:T(8,128)(2,1)}), bf16[4096,1536]{0,1:T(8,128)(2,1)}) %all-gather.2.cloned.1.call-update) | async-done | bytes 12582928 | tf_op jit(solution)/shard_map/all_gather | solution.py:32
  205.5 10.2 %fusion.6 = f32[4096,256]{1,0:T(8,128)} fusion(bf16[4096,1536]{0,1:T(8,128)(2,1)} %all-gather.2.cloned.1.call-done, bf16[256,1536]{1,0:T(8,128)(2,1)S(1)} %bitcast.22), kind=kOutput, calls=%fused_computation.13 | convolution fusion | flops 3221225472 | bytes 17563648 | tf_op jit(solution)/shard_map/dot_general | solution.py:34
  215.8 0.0 reduce-scatter.2.cloned.1.call-update
  215.8 88.0 %reduce-scatter.2.cloned.1.call-done = f32[256,256]{1,0:T(8,128)} async-done(((f32[4096,256]{1,0:T(8,128)}), f32[256,256]{1,0:T(8,128)}) %reduce-scatter.2.cloned.1.call-update) | async-done | bytes 262160 | tf_op jit(solution)/shard_map/reduce_scatter | solution.py:33
  303.8 1.7 broadcast_multiply_fusion
  (1 shorter events, 0.0 us)
Async XLA Ops:
  6.5 46.3 %copy-start = (bf16[2,6,128,128]{3,2,1,0:T(8,128)(2,1)S(1)}, bf16[2,6,128,128]{3,2,1,0:T(8,128)(2,1)}, u32[]{:S(2)}) copy-start(bf16[2,6,128,128]{3,2,1,0:T(8,128)(2,1)} %param.4) | copy-start | bytes 1179652
  6.5 199.0 %all-gather.2.cloned.1.call-start = ((), (), s32[]{:S(2)}) async-start(), calls=%async_computation.1 | async-start | bytes 13369344 | tf_op jit(solution)/shard_map/all_gather | solution.py:32
  55.6 248.2 %reduce-scatter.2.cloned.1.call-start = ((), (), s32[]{:S(2)}) async-start(), calls=%async_computation.2 | async-start | bytes 4456448 | tf_op jit(solution)/shard_map/reduce_scatter | solution.py:33
Sparse Core Ops, SparseCore 0:
  55.7 149.7 all-gather.1
  215.9 87.8 reduce-scatter.1
where the time goes:
time: 313 us; the launch traced here: 312 us
  waiting for transfers between devices  238 us (76%)
  blocking collectives  44.8 us (14%)
  between operations  13.4 us (4%)
  matrix products  11.2 us (4%)
    all_gather x1, waiting for transfers between devices, local(): gathered = lax.all_gather(dense, 'row', axis=0, tiled=True)  150 us
    reduce_scatter x1, waiting for transfers between devices, local(): lax.psum_scatter(jnp.dot(gathered, dense.T, preferred_element_type=jnp.fl...  88 us
    all_gather x1, blocking collectives, local(): full_metric = lax.all_gather(metric, 'row', axis=1, tiled=True)  44.8 us
    dot_general x1, matrix products, local(): jnp.dot(gathered, dense.T, preferred_element_type=jnp.float32)  10.2 us
  transfers between devices with their start and end apart: 2, of which 2 were waited for; matrix products, arithmetic and copies ran while one was open for 0% of the time, Pallas kernels for 0%

commit v1 on v0

--- a/solution.py
+++ b/solution.py
@@ -20,7 +20,15 @@
 def local(fit_tiles, aux_list, aux_count, metric):
     slots = fit_tiles.shape[1]
     local_aux = metric.shape[0]
-    full_metric = lax.all_gather(metric, "row", axis=1, tiled=True)
+    full_metric = jnp.concatenate(
+        lax.all_to_all(
+            jnp.stack(lax.axis_size("row") * [metric], 0),
+            split_axis=0,
+            axis_name="row",
+            concat_axis=0,
+        ),
+        1,
+    )
     alive = jnp.arange(slots, dtype=jnp.int32)[None, :] < aux_count
     marked = jnp.where(alive, aux_list, local_aux)
     picked = full_metric[aux_list]

time: 313 us -> 291 us (0.930)
  blocking collectives: 44.8 us -> 0 us
  starting transfers between devices: 0.04 us -> 11.6 us
  waiting for transfers between devices: 238 us -> 248 us
    all_gather x1 -> x0, blocking collectives: 44.8 us -> none  [local(): full_metric = lax.all_gather(metric, 'row', axis=1, tiled=True)]
    all_to_all x0 -> x1, waiting for transfers between devices: none -> 13 us  [local(): lax.all_to_all(jnp.stack(lax.axis_size('row') * [metric], 0), split_axis=...]
    all_to_all x0 -> x1, starting transfers between devices: none -> 11.6 us  [local(): lax.all_to_all(jnp.stack(lax.axis_size('row') * [metric], 0), split_axis=...]
  transfers between devices with their start and end apart: 2 -> 3, of which waited for: 2 -> 3; matrix products, arithmetic and copies ran while one was open for 0% -> 0% of each run, Pallas kernels for 0% -> 0%
where the time goes in v1:
time: 291 us
  waiting for transfers between devices  248 us (85%)
  between operations  13.5 us (5%)
  starting transfers between devices  11.6 us (4%)
  matrix products  11.2 us (4%)
  local copies, waits for them, and re-layouts  4.12 us (1%)
    all_gather x1, waiting for transfers between devices, local(): gathered = lax.all_gather(dense, 'row', axis=0, tiled=True)  147 us
    reduce_scatter x1, waiting for transfers between devices, local(): lax.psum_scatter(jnp.dot(gathered, dense.T, preferred_element_type=jnp.fl...  88.2 us
    all_to_all x1, waiting for transfers between devices, local(): lax.all_to_all(jnp.stack(lax.axis_size('row') * [metric], 0), split_axis=...  13 us
    all_to_all x1, starting transfers between devices, local(): lax.all_to_all(jnp.stack(lax.axis_size('row') * [metric], 0), split_axis=...  11.6 us
    dot_general x1, matrix products, local(): jnp.dot(gathered, dense.T, preferred_element_type=jnp.float32)  10.2 us
  transfers between devices with their start and end apart: 3, of which 3 were waited for; matrix products, arithmetic and copies ran while one was open for 0% of the time, Pallas kernels for 0%

profile of v1, /device:TPU:8, one launch (start us, length us, event | category | flops | bytes accessed | tf_op | source)
XLA Modules:
  0.0 291.0 jit_solution(8231469806074784128)
XLA Ops:
  6.5 0.0 copy-start
  6.5 1.6 stack.2
  8.1 11.6 %all-to-all-start = ((bf16[16,12,8,128]{3,2,1,0:T(8,128)(2,1)}), bf16[16,12,8,128]{3,2,1,0:T(8,128)(2,1)S(1)}, u32[]{:S(2)}, u32[]{:S(2)}) async-start(bf16[16,12,8,128]{3,2,1,0:T(8,128)(2,1)} %stack.2), calls=%async_computation | async-start | bytes 786432 | tf_op jit(solution)/shard_map/all_to_all | solution.py:24
  19.7 0.0 all-gather.2.cloned.1.call-start
  19.7 0.8 compare_select_fusion.1
  20.5 0.1 reshape.17
  20.6 13.0 %all-to-all-done = bf16[16,12,8,128]{3,2,1,0:T(8,128)(2,1)S(1)} async-done(((bf16[16,12,8,128]{3,2,1,0:T(8,128)(2,1)}), bf16[16,12,8,128]{3,2,1,0:T(8,128)(2,1)S(1)}, u32[]{:S(2)}, u32[]{:S(2)}) %all-to-all-start) | async-done | bytes 393248 | tf_op jit(solution)/shard_map/all_to_all | solution.py:24
  33.5 0.1 copy.17
  33.6 0.6 gather_fusion
  34.3 0.0 copy-done
  34.3 0.4 fusion
  34.7 0.3 copy.8
  35.0 0.5 convolution_convert_fusion
  35.6 0.2 copy.16
  35.8 1.2 copy.12
  37.0 0.0 all-gather.2.cloned.1.call-update
  37.0 0.0 reduce-scatter.2.cloned.1.call-start
  37.1 147.0 %all-gather.2.cloned.1.call-done = bf16[4096,1536]{0,1:T(8,128)(2,1)} async-done(((bf16[256,1536]{0,1:T(8,128)(2,1)}), bf16[4096,1536]{0,1:T(8,128)(2,1)}) %all-gather.2.cloned.1.call-update) | async-done | bytes 12582928 | tf_op jit(solution)/shard_map/all_gather | solution.py:40
  184.1 10.2 %fusion.4 = f32[4096,256]{1,0:T(8,128)} fusion(bf16[4096,1536]{0,1:T(8,128)(2,1)} %all-gather.2.cloned.1.call-done, bf16[256,1536]{1,0:T(8,128)(2,1)S(1)} %bitcast.27), kind=kOutput, calls=%fused_computation.13 | convolution fusion | flops 3221225472 | bytes 17563648 | tf_op jit(solution)/shard_map/dot_general | solution.py:42
  194.3 0.0 reduce-scatter.2.cloned.1.call-update
  194.3 88.2 %reduce-scatter.2.cloned.1.call-done = f32[256,256]{1,0:T(8,128)} async-done(((f32[4096,256]{1,0:T(8,128)}), f32[256,256]{1,0:T(8,128)}) %reduce-scatter.2.cloned.1.call-update) | async-done | bytes 262160 | tf_op jit(solution)/shard_map/reduce_scatter | solution.py:41
  282.5 1.7 broadcast_multiply_fusion
  (1 shorter events, 0.0 us)
Async XLA Ops:
  6.5 27.7 %copy-start = (bf16[2,6,128,128]{3,2,1,0:T(8,128)(2,1)S(1)}, bf16[2,6,128,128]{3,2,1,0:T(8,128)(2,1)}, u32[]{:S(2)}) copy-start(bf16[2,6,128,128]{3,2,1,0:T(8,128)(2,1)} %param.4) | copy-start | bytes 1179652
  8.1 25.4 %all-to-all-start = ((bf16[16,12,8,128]{3,2,1,0:T(8,128)(2,1)}), bf16[16,12,8,128]{3,2,1,0:T(8,128)(2,1)S(1)}, u32[]{:S(2)}, u32[]{:S(2)}) async-start(bf16[16,12,8,128]{3,2,1,0:T(8,128)(2,1)} %stack.2), calls=%async_computation | async-start | bytes 786432 | tf_op jit(solution)/shard_map/all_to_all | solution.py:24
  19.7 164.4 %all-gather.2.cloned.1.call-start = ((), (), s32[]{:S(2)}) async-start(), calls=%async_computation.2 | async-start | bytes 13369344 | tf_op jit(solution)/shard_map/all_gather | solution.py:40
  37.0 245.5 %reduce-scatter.2.cloned.1.call-start = ((), (), s32[]{:S(2)}) async-start(), calls=%async_computation.3 | async-start | bytes 4456448 | tf_op jit(solution)/shard_map/reduce_scatter | solution.py:41
Sparse Core Ops, SparseCore 0:
  37.1 146.9 all-gather.1
  194.4 87.9 reduce-scatter.1
